TPU v7x, 1024 devices: a whole 8x8x8 slice. The times are simulated.
1024 devices in a mesh: pw: 8 (over z_hi, core), band: 128 (over x, z_lo, y).
Axes of the slice: x: 8, y: 8, z: 8 (z_hi: 4, z_lo: 2; z = z_hi * 2 + z_lo), core: 2. Of those that a mesh axis runs over, the one named last changes fastest.
Arguments:
- wavefunctions: float32 [16384, 8192], P('pw', 'band'), may hold values from -6 to 6
- projectors: float32 [16384, 1024], P('pw', 'band'), may hold values from -0.046875 to 0.046875
- coupling: float32 [4, 256, 256], replicated, may hold values from -1.5 to 1.5
- block_type: int32 [4], replicated, may hold values from 0 to 3
Outputs:
- applied: float32 [16384, 8192], P('pw', 'band')
All inputs are finite; a program needn't handle non-finite values.
Results may differ from a plain program's by a relative error of at most 0.000071.
Values sent between devices are 32-bit elements; how exact they have to be, the bound alone decides.
No kernel may reach another device: no remote copies, remote signals or barrier semaphores. Data moves between devices by JAX's collectives and lax.ppermute only.
A program may use at most 32 MiB of HBM per device.

v0:
```python
import jax
import jax.numpy as jnp
from jax import lax
from jax.sharding import PartitionSpec as P


def couple(blocks, projections):
    columns = projections.shape[1]
    grouped = projections.reshape(blocks.shape[0], blocks.shape[1], columns)
    mixed = jnp.einsum("cij,cjb->cib", blocks, grouped, precision=lax.Precision.HIGHEST)
    return mixed.reshape(blocks.shape[0] * blocks.shape[1], columns)


def local(wavefunctions, projectors, coupling, block_type):
    types = coupling.shape[0]
    onehot = (block_type[:, None] == jnp.arange(types, dtype=jnp.int32)[None, :]).astype(
        jnp.float32
    )
    blocks = jnp.einsum("ct,tij->cij", onehot, coupling, precision=lax.Precision.HIGHEST)
    gathered = lax.all_gather(projectors, "band", axis=1, tiled=True)
    partial_value = lax.dot_general(
        gathered,
        wavefunctions,
        (((0,), (0,)), ((), ())),
        precision=lax.Precision.HIGHEST,
        preferred_element_type=jnp.float32,
    )
    projections = lax.psum(partial_value, "pw")
    coupled = couple(blocks, projections)
    return wavefunctions + jnp.dot(
        gathered, coupled, precision=lax.Precision.HIGHEST, preferred_element_type=jnp.float32
    )


def solution(mesh):
    return jax.shard_map(
        local,
        mesh=mesh,
        in_specs=(P("pw", "band"), P("pw", "band"), P(), P()),
        out_specs=P("pw", "band"),
        check_vma=False,
    )
```

profile of v0, /device:TPU:1, one launch (start us, length us, event | category | flops | bytes accessed | tf_op | source)
XLA Modules:
  0.0 730.7 jit_solution(5328182397328889359)
XLA Ops:
  6.5 0.0 copy-start
  6.5 0.0 copy-start.1
  6.5 0.0 copy-start.2
  6.5 0.0 all-gather.2.cloned.1.call-start
  6.5 0.7 all-gather.2.cloned.1.call-update
  7.3 0.0 all-reduce.2.cloned.1.call-start
  7.3 521.9 %all-gather.2.cloned.1.call-done = f32[2048,1024]{0,1:T(8,128)} async-done(((f32[2048,8]{0,1:T(8,128)}), f32[2048,1024]{0,1:T(8,128)}) %all-gather.2.cloned.1.call-update) | async-done | bytes 8388624 | tf_op jit(solution)/shard_map/all_gather | solution.py:20
  529.2 10.6 %fusion.7 = f32[1024,64]{0,1:T(8,128)S(1)} fusion(f32[2048,1024]{0,1:T(8,128)} %all-gather.2.cloned.1.call-done, f32[2048,64]{0,1:T(8,128)} %param.4), kind=kOutput, calls=%fused_computation.10 | convolution fusion | flops 1610612736 | bytes 9175040 | tf_op jit(solution)/shard_map/dot_general | solution.py:21
  539.8 0.7 copy.17
  540.6 0.0 all-reduce.2.cloned.1.call-update
  540.6 0.0 copy-done
  540.6 0.0 copy-done.2
  540.6 1.7 fusion.2
  542.3 171.1 %all-reduce.2.cloned.1.call-done = f32[4,256,64]{1,2,0:T(8,128)} async-done(((f32[4,256,64]{1,2,0:T(8,128)}), f32[4,256,64]{1,2,0:T(8,128)}) %all-reduce.2.cloned.1.call-update) | async-done | bytes 262160 | tf_op jit(solution)/shard_map/psum | solution.py:28
  713.3 2.2 convolution_bitcast_fusion.1
  715.5 0.0 copy-done.1
  715.5 8.3 %fusion = f32[2048,64]{0,1:T(8,128)} fusion(f32[2048,64]{0,1:T(8,128)S(1)} %copy-done.1, f32[1024,64]{0,1:T(8,128)S(1)} %bitcast.19, f32[2048,1024]{0,1:T(8,128)} %all-gather.2.cloned.1.call-done), kind=kOutput, calls=%fused_computation.1 | convolution fusion | flops 1610743808 | bytes 9699328 | tf_op jit(solution)/shard_map/dot_general | solution.py:30
  (1 shorter events, 0.0 us)
Async XLA Ops:
  6.5 534.1 %copy-start = (f32[4,256,256]{2,1,0:T(8,128)S(1)}, f32[4,256,256]{2,1,0:T(8,128)}, u32[]{:S(2)}) copy-start(f32[4,256,256]{2,1,0:T(8,128)} %param.6) | copy-start | bytes 3145732
  6.5 709.0 %copy-start.1 = (f32[2048,64]{0,1:T(8,128)S(1)}, f32[2048,64]{0,1:T(8,128)}, u32[]{:S(2)}) copy-start(f32[2048,64]{0,1:T(8,128)} %param.4) | copy-start | bytes 1572868
  6.5 534.1 %copy-start.2 = (s32[4]{0:T(128)S(1)}, s32[4]{0:T(128)}, u32[]{:S(2)}) copy-start(s32[4]{0:T(128)} %param.7) | copy-start | bytes 52
  6.5 522.7 %all-gather.2.cloned.1.call-start = ((), (), s32[]{:S(2)}) async-start(), calls=%async_computation | async-start | bytes 8454144 | tf_op jit(solution)/shard_map/all_gather | solution.py:20
  7.3 706.1 %all-reduce.2.cloned.1.call-start = ((), (), s32[]{:S(2)}) async-start(), calls=%async_computation.1 | async-start | bytes 524288 | tf_op jit(solution)/shard_map/psum | solution.py:28
Sparse Core Ops, SparseCore 0:
  10.0 519.1 all-gather.1
  540.7 172.5 all-reduce.1
where the time goes:
time: 731 us
  waiting for transfers between devices  694 us (95%)
  matrix products  22.8 us (3%)
  between operations  13.5 us (2%)
    all_gather x1, waiting for transfers between devices, local(): gathered = lax.all_gather(projectors, 'band', axis=1, tiled=True)  522 us
    psum x1, waiting for transfers between devices, local(): projections = lax.psum(partial_value, 'pw')  171 us
  transfers between devices with their start and end apart: 2, of which 2 were waited for; matrix products, arithmetic and copies ran while one was open for 0% of the time, Pallas kernels for 0%

commit v1 on v0

v1 whole, which is shorter than its diff:
```python
import jax
import jax.numpy as jnp
from jax import lax
from jax.sharding import PartitionSpec as P

PREC = lax.Precision.HIGH


def dot(a, b, dims):
    return lax.dot_general(
        a, b, (dims, ((), ())), precision=PREC, preferred_element_type=jnp.float32
    )


def exact(a, b, dims):
    return lax.dot_general(
        a,
        b,
        (dims, ((), ())),
        precision=lax.Precision.HIGHEST,
        preferred_element_type=jnp.float32,
    )


def make_local(npw, nband, nx, nzl, ny):
    plane = [
        [x * nzl * ny + z * ny + y for x in range(nx) for y in range(ny)] for z in range(nzl)
    ]
    swap = [(i, i ^ ny) for i in range(nband)]

    def local(wavefunctions, projectors, coupling, block_type):
        types, block, _ = coupling.shape
        nblocks = block_type.shape[0]
        wt = wavefunctions.T
        pt = projectors.T
        bands, rows = wt.shape
        mine = pt.shape[0]
        z_lo = (lax.axis_index("band") // ny) % nzl

        other = lax.ppermute(pt, "band", swap)
        both = jnp.where(
            z_lo == 0, jnp.concatenate([pt, other]), jnp.concatenate([other, pt])
        )
        gathered = lax.all_gather(both, "band", axis=0, axis_index_groups=plane, tiled=True)

        nproj = gathered.shape[0]
        at = jnp.arange(block, dtype=jnp.int32)
        j, y, z, outer = (
            at % mine,
            (at // (nzl * mine)) % ny,
            (at // mine) % nzl,
            at // (nzl * ny * mine),
        )
        source = ((outer * nzl + z) * ny + y) * mine + j
        pick = (source[:, None] == at[None, :]).astype(jnp.float32)
        chosen = []
        for i in range(nblocks):
            v = lax.dynamic_index_in_dim(coupling, block_type[i], 0, keepdims=False)
            v = exact(pick, v, ((1,), (0,)))
            chosen.append(exact(v, pick, ((1,), (1,))))

        part = dot(wt, gathered, ((1,), (1,)))
        split = lax.all_to_all(part.reshape(npw, bands // npw, nproj), "pw", 0, 0)
        proj = jnp.sum(split, axis=0)
        coupled = jnp.concatenate(
            [
                dot(proj[:, i * block : (i + 1) * block], chosen[i], ((1,), (1,)))
                for i in range(nblocks)
            ],
            axis=1,
        )
        full = lax.all_to_all(
            jnp.broadcast_to(coupled[None], (npw,) + coupled.shape), "pw", 0, 0
        ).reshape(bands, nproj)
        out = wt + dot(full, gathered, ((1,), (0,)))
        return out.T

    return local


def solution(mesh):
    npw, nband = mesh.shape["pw"], mesh.shape["band"]
    local = make_local(npw, nband, 8, 2, 8)
    return jax.shard_map(
        local,
        mesh=mesh,
        in_specs=(P("pw", "band"), P("pw", "band"), P(), P()),
        out_specs=P("pw", "band"),
        check_vma=False,
    )
```

time: 731 us -> 188 us (0.26)
  waiting for transfers between devices: 694 us -> 114 us
  blocking collectives: 0 us -> 15.1 us
  starting transfers between devices: 0.04 us -> 14.8 us
  between operations: 13.5 us -> 21.4 us
    all_gather x1, waiting for transfers between devices: 522 us -> 103 us  [local(): lax.all_gather(both, 'band', axis=0, axis_index_groups=plane, tiled=True)]
    psum x1 -> x0, waiting for transfers between devices: 171 us -> none  [local(): projections = lax.psum(partial_value, 'pw')]
    all_to_all x0 -> x1, blocking collectives: none -> 15.1 us  [local(): lax.all_to_all(jnp.broadcast_to(coupled[None], (npw,) + coupled.shape), '...]
    all_to_all x0 -> x1, waiting for transfers between devices: none -> 9.16 us  [local(): split = lax.all_to_all(part.reshape(npw, bands // npw, nproj), 'pw', 0, 0)]
    all_to_all x0 -> x1, starting transfers between devices: none -> 8.94 us  [local(): split = lax.all_to_all(part.reshape(npw, bands // npw, nproj), 'pw', 0, 0)]
    dot_general x4 -> x14, matrix products: 22.8 us -> 18.6 us  [the longest x6 15.7 us: dot(): lax.dot_general(a, b, (dims, ((), ())), precision=PREC, preferred_element...]
  transfers between devices with their start and end apart: 2 -> 3, of which waited for: 2 -> 3; matrix products, arithmetic and copies ran while one was open for 0% -> 2% of each run, Pallas kernels for 0% -> 0%
where the time goes in v1:
time: 188 us; the launch traced here: 187 us
  waiting for transfers between devices  114 us (61%)
  between operations  21.4 us (11%)
  matrix products  18.6 us (10%)
  blocking collectives  15.1 us (8%)
  starting transfers between devices  14.8 us (8%)
    all_gather x1, waiting for transfers between devices, local(): lax.all_gather(both, 'band', axis=0, axis_index_groups=plane, tiled=True)  103 us
    dot_general x6, matrix products, dot(): lax.dot_general(a, b, (dims, ((), ())), precision=PREC, preferred_element...  15.7 us
    all_to_all x1, blocking collectives, local(): lax.all_to_all(jnp.broadcast_to(coupled[None], (npw,) + coupled.shape), '...  15.1 us
    all_to_all x1, waiting for transfers between devices, local(): split = lax.all_to_all(part.reshape(npw, bands // npw, nproj), 'pw', 0, 0)  9.16 us
    all_to_all x1, starting transfers between devices, local(): split = lax.all_to_all(part.reshape(npw, bands // npw, nproj), 'pw', 0, 0)  8.94 us
    ppermute x1, starting transfers between devices, local(): other = lax.ppermute(pt, 'band', swap)  5.85 us
  transfers between devices with their start and end apart: 3, of which 3 were waited for; matrix products, arithmetic and copies ran while one was open for 2% of the time, Pallas kernels for 0%

profile of v1, /device:TPU:1, one launch (start us, length us, event | category | flops | bytes accessed | tf_op | source)
XLA Modules:
  0.0 187.2 jit_solution(17950510272970659148)
XLA Ops:
  6.5 5.8 %collective-permute-start = (f32[8,2048]{1,0:T(8,128)}, f32[8,2048]{1,0:T(8,128)S(1)}, u32[]{:S(2)}, u32[]{:S(2)}) collective-permute-start(f32[8,2048]{1,0:T(8,128)} %bitcast.35), channel_id=1, source_target_pairs={{0,8},{1,9},{2,10},{3,11},{4,12},{5,13},{6,14},{7,15},{8,0},{9,1},... | collective-permute-start | bytes 196616 | tf_op jit(solution)/shard_map/ppermute | solution.py:40
  12.4 1.8 collective-permute-done
  14.2 1.6 maximum_select_fusion
  15.8 0.0 all-gather.2.cloned.1.call-update
  15.9 1.5 fusion.48
  25.2 0.3 fusion.3
  25.5 0.3 fusion.5
  25.8 0.3 fusion.7
  26.2 0.4 fusion.14
  26.6 0.4 fusion.15
  27.0 0.4 fusion.16
  27.4 103.1 %all-gather.2.cloned.1.call-done = f32[1024,2048]{1,0:T(8,128)} async-done(((f32[16,2048]{1,0:T(8,128)}), f32[1024,2048]{1,0:T(8,128)}) %all-gather.2.cloned.1.call-update) | async-done | bytes 8388624 | tf_op jit(solution)/shard_map/all_gather | solution.py:44
  130.6 8.1 %convolution_bitcast_fusion = f32[8,8,1024]{2,1,0:T(8,128)} fusion(f32[1024,2048]{1,0:T(8,128)} %all-gather.2.cloned.1.call-done, f32[2048,64]{0,1:T(8,128)} %param.4), kind=kOutput, calls=%fused_computation.1 | convolution fusion | flops 805306368 | bytes 9175040 | tf_op jit(solution)/shard_map/dot_general | solution.py:10
  138.6 8.9 %all-to-all-start = ((f32[8,8,1024]{2,1,0:T(8,128)}), f32[8,8,1024]{2,1,0:T(8,128)S(1)}, u32[]{:S(2)}, u32[]{:S(2)}) async-start(f32[8,8,1024]{2,1,0:T(8,128)} %convolution_bitcast_fusion), calls=%async_computation | async-start | bytes 524288 | tf_op jit(solution)/shard_map/all_to_all | solution.py:63
  147.6 0.3 fusion.1
  147.9 0.4 fusion.13
  148.3 9.2 %all-to-all-done = f32[8,8,1024]{2,1,0:T(8,128)S(1)} async-done(((f32[8,8,1024]{2,1,0:T(8,128)}), f32[8,8,1024]{2,1,0:T(8,128)S(1)}, u32[]{:S(2)}, u32[]{:S(2)}) %all-to-all-start) | async-done | bytes 262176 | tf_op jit(solution)/shard_map/all_to_all | solution.py:63
  157.5 0.2 fusion.27
  157.7 0.3 fusion.29
  157.9 0.3 fusion.31
  158.2 0.3 fusion.25
  158.5 0.1 broadcast_in_dim.2
  158.6 15.1 %all_to_all.10 = f32[8,8,1024]{2,1,0:T(8,128)S(1)} all-to-all(f32[8,8,1024]{2,1,0:T(8,128)S(1)} %broadcast_in_dim.2), channel_id=1, replica_groups=mesh['pw'=8,'band'=128] {'pw'}, dimensions={0} | all-to-all | bytes 524288 | tf_op jit(solution)/shard_map/all_to_all | solution.py:72
  173.7 6.7 %convolution_add_fusion = f32[2048,64]{0,1:T(8,128)} fusion(f32[2048,64]{0,1:T(8,128)S(1)} %copy-done.1, f32[1024,2048]{1,0:T(8,128)} %all-gather.2.cloned.1.call-done, f32[8,8,1024]{2,1,0:T(8,128)S(1)} %all_to_all.10), kind=kOutput, calls=%fused_computation | convolution fusion | flops 805437440 | bytes 9699328 | tf_op jit(solution)/shard_map/dot_general | solution.py:10
  (8 shorter events, 0.0 us)
Async XLA Ops:
  6.5 18.6 %copy-start = (f32[4,256,256]{2,1,0:T(8,128)S(1)}, f32[4,256,256]{2,1,0:T(8,128)}, u32[]{:S(2)}) copy-start(f32[4,256,256]{2,1,0:T(8,128)} %param.6) | copy-start | bytes 3145732
  6.5 167.2 %copy-start.1 = (f32[2048,64]{0,1:T(8,128)S(1)}, f32[2048,64]{0,1:T(8,128)}, u32[]{:S(2)}) copy-start(f32[2048,64]{0,1:T(8,128)} %param.4) | copy-start | bytes 1572868
  6.5 124.1 %all-gather.2.cloned.1.call-start = ((), (), s32[]{:S(2)}) async-start(), calls=%async_computation.2 | async-start | bytes 8519680 | tf_op jit(solution)/shard_map/all_gather | solution.py:44
  6.5 7.7 %collective-permute-start = (f32[8,2048]{1,0:T(8,128)}, f32[8,2048]{1,0:T(8,128)S(1)}, u32[]{:S(2)}, u32[]{:S(2)}) collective-permute-start(f32[8,2048]{1,0:T(8,128)} %bitcast.35), channel_id=1, source_target_pairs={{0,8},{1,9},{2,10},{3,11},{4,12},{5,13},{6,14},{7,15},{8,0},{9,1},... | collective-permute-start | bytes 196616 | tf_op jit(solution)/shard_map/ppermute | solution.py:40
  138.6 18.8 %all-to-all-start = ((f32[8,8,1024]{2,1,0:T(8,128)}), f32[8,8,1024]{2,1,0:T(8,128)S(1)}, u32[]{:S(2)}, u32[]{:S(2)}) async-start(f32[8,8,1024]{2,1,0:T(8,128)} %convolution_bitcast_fusion), calls=%async_computation | async-start | bytes 524288 | tf_op jit(solution)/shard_map/all_to_all | solution.py:63
Sparse Core Ops, SparseCore 0:
  16.0 114.5 all-gather.1

commit v2 on v0

v2 whole, which is shorter than its diff:
```python
import jax
import jax.numpy as jnp
from jax import lax
from jax.sharding import PartitionSpec as P


def dot(a, b, dims, precision=lax.Precision.HIGH):
    return lax.dot_general(
        a, b, (dims, ((), ())), precision=precision, preferred_element_type=jnp.float32
    )


def make_local(npw, nx, nzl, ny):
    nband = nx * nzl * ny

    def at(x, z, y):
        return (x * nzl + z) * ny + y

    along_y = [[at(x, z, y) for y in range(ny)] for x in range(nx) for z in range(nzl)]
    along_x = [[at(x, z, y) for x in range(nx)] for z in range(nzl) for y in range(ny)]
    column = [
        [p * nband + at(x, z, y) for z in range(nzl) for p in range(npw)]
        for x in range(nx)
        for y in range(ny)
    ]
    swap = [(i, i ^ ny) for i in range(nband)]
    both = ("pw", "band")

    def local(wavefunctions, projectors, coupling, block_type):
        block = coupling.shape[1]
        nblocks = block_type.shape[0]
        wt = wavefunctions.T
        pt = projectors.T
        bands, rows = wt.shape
        mine = pt.shape[0]
        first = (lax.axis_index("band") // ny) % nzl == 0
        members = nzl * npw

        line = lax.all_to_all(
            jnp.broadcast_to(pt[None], (ny, mine, rows)), "band", 0, 0, axis_index_groups=along_y
        ).reshape(ny * mine, rows)
        gathered = lax.all_gather(line, "band", axis=0, axis_index_groups=along_x, tiled=True)
        held = gathered.shape[0]

        other = lax.ppermute(wt, "band", swap)
        pair = jnp.where(first, jnp.concatenate([wt, other]), jnp.concatenate([other, wt]))

        piece = block // nzl
        spot = jnp.arange(block, dtype=jnp.int32)
        z, outer, inner = spot // piece, (spot % piece) // (ny * mine), spot % (ny * mine)
        source = (outer * nzl + z) * (ny * mine) + inner
        pick = (source[:, None] == spot[None, :]).astype(jnp.float32)
        mixers = []
        for i in range(nblocks):
            v = lax.dynamic_index_in_dim(coupling, block_type[i], 0, keepdims=False)
            v = dot(pick, v, ((1,), (0,)), lax.Precision.HIGHEST)
            mixers.append(dot(v, pick, ((1,), (1,)), lax.Precision.HIGHEST))

        part = dot(pair, gathered, ((1,), (1,)))
        few = nzl * bands // members
        split = lax.all_to_all(
            part.reshape(members, few, held), both, 0, 0, axis_index_groups=column
        )
        proj = jnp.sum(split.reshape(nzl, npw, few, held), axis=1)
        coupled = []
        for i in range(nblocks):
            own = [proj[z, :, i * piece : (i + 1) * piece] for z in range(nzl)]
            coupled.append(dot(jnp.concatenate(own, axis=1), mixers[i], ((1,), (1,))))
        back = jnp.stack(
            [
                jnp.concatenate([c[:, z * piece : (z + 1) * piece] for c in coupled], axis=1)
                for z in range(nzl)
            ]
        )
        back = jnp.broadcast_to(back[:, None], (nzl, npw, few, held)).reshape(members, few, held)
        full = lax.all_to_all(back, both, 0, 0, axis_index_groups=column).reshape(
            nzl * bands, held
        )
        low, high = full[:bands], full[bands:]
        sent = dot(jnp.where(first, high, low), gathered, ((1,), (0,)))
        received = lax.ppermute(sent, "band", swap)
        kept = wt + dot(jnp.where(first, low, high), gathered, ((1,), (0,)))
        return (lax.optimization_barrier(kept) + received).T

    return local


def solution(mesh):
    nx, nzl, ny = 8, 2, 8
    local = make_local(mesh.shape["pw"], nx, nzl, ny)
    return jax.shard_map(
        local,
        mesh=mesh,
        in_specs=(P("pw", "band"), P("pw", "band"), P(), P()),
        out_specs=P("pw", "band"),
        check_vma=False,
    )
```

time: 731 us -> 167 us (0.23)
  waiting for transfers between devices: 694 us -> 73.2 us
  blocking collectives: 0 us -> 34.6 us
  starting transfers between devices: 0.04 us -> 19.8 us
  matrix products: 22.8 us -> 14.2 us
  between operations: 13.5 us -> 21.2 us
    all_gather x1, waiting for transfers between devices: 522 us -> 51 us  [local(): lax.all_gather(line, 'band', axis=0, axis_index_groups=along_x, tiled=True)]
    psum x1 -> x0, waiting for transfers between devices: 171 us -> none  [local(): projections = lax.psum(partial_value, 'pw')]
    all_to_all x0 -> x2, blocking collectives: none -> 34.6 us  [the longest x1 20.1 us: local(): lax.all_to_all(jnp.broadcast_to(pt[None], (ny, mine, rows)), 'band', 0, 0...]
    ppermute x0 -> x2, waiting for transfers between devices: none -> 11.5 us  [the longest x1 11.5 us: local(): received = lax.ppermute(sent, 'band', swap)]
    ppermute x0 -> x2, starting transfers between devices: none -> 10.9 us  [the longest x1 8.88 us: local(): other = lax.ppermute(wt, 'band', swap)]
    all_to_all x0 -> x1, waiting for transfers between devices: none -> 10.7 us  [local(): lax.all_to_all(part.reshape(members, few, held), both, 0, 0, axis_index_g...]
    all_to_all x0 -> x1, starting transfers between devices: none -> 8.96 us  [local(): lax.all_to_all(part.reshape(members, few, held), both, 0, 0, axis_index_g...]
    dot_general x4 -> x15, matrix products: 22.8 us -> 14.2 us  [dot(): lax.dot_general(a, b, (dims, ((), ())), precision=precision, preferred_el...]
  transfers between devices with their start and end apart: 2 -> 4, of which waited for: 2 -> 3; matrix products, arithmetic and copies ran while one was open for 0% -> 4% of each run, Pallas kernels for 0% -> 0%
where the time goes in v2:
time: 167 us; the launch traced here: 166 us
  waiting for transfers between devices  73.2 us (44%)
  blocking collectives  34.6 us (21%)
  between operations  21.2 us (13%)
  starting transfers between devices  19.8 us (12%)
  matrix products  14.2 us (9%)
  local copies, waits for them, and re-layouts  2.5 us (1%)
    all_gather x1, waiting for transfers between devices, local(): lax.all_gather(line, 'band', axis=0, axis_index_groups=along_x, tiled=True)  51 us
    all_to_all x1, blocking collectives, local(): lax.all_to_all(jnp.broadcast_to(pt[None], (ny, mine, rows)), 'band', 0, 0...  20.1 us
    all_to_all x1, blocking collectives, local(): lax.all_to_all(back, both, 0, 0, axis_index_groups=column)  14.5 us
    dot_general x15, matrix products, dot(): lax.dot_general(a, b, (dims, ((), ())), precision=precision, preferred_el...  14.2 us
    ppermute x1, waiting for transfers between devices, local(): received = lax.ppermute(sent, 'band', swap)  11.5 us
    all_to_all x1, waiting for transfers between devices, local(): lax.all_to_all(part.reshape(members, few, held), both, 0, 0, axis_index_g...  10.7 us
    all_to_all x1, starting transfers between devices, local(): lax.all_to_all(part.reshape(members, few, held), both, 0, 0, axis_index_g...  8.96 us
    ppermute x1, starting transfers between devices, local(): other = lax.ppermute(wt, 'band', swap)  8.88 us
  transfers between devices with their start and end apart: 4, of which 3 were waited for; matrix products, arithmetic and copies ran while one was open for 4% of the time, Pallas kernels for 0%

profile of v2, /device:TPU:1, one launch (start us, length us, event | category | flops | bytes accessed | tf_op | source)
XLA Modules:
  0.0 166.5 jit_solution(11660110724062068854)
XLA Ops:
  6.5 1.0 broadcast_in_dim.4
  7.5 20.1 %all_to_all.15 = f32[8,8,2048]{2,1,0:T(8,128)} all-to-all(f32[8,8,2048]{2,1,0:T(8,128)S(1)} %broadcast_in_dim.4), channel_id=1, replica_groups={{0,1,2,3,4,5,6,7},{8,9,10,11,12,13,14,15},{16,17,18,19,20,21,22,23},{24..., dimensions={0} | all-to-all | bytes 1048576 | tf_op jit(solution)/shard_map/all_to_all | solution.py:39
  27.7 8.9 %collective-permute-start = (f32[64,2048]{1,0:T(8,128)}, f32[64,2048]{1,0:T(8,128)S(1)}, u32[]{:S(2)}, u32[]{:S(2)}) collective-permute-start(f32[64,2048]{1,0:T(8,128)} %bitcast.65), channel_id=1, source_target_pairs={{0,8},{1,9},{2,10},{3,11},{4,12},{5,13},{6,14},{7,15},{8,0},{9,1},... | collective-permute-start | bytes 1572872 | tf_op jit(solution)/shard_map/ppermute | solution.py:45
  36.6 1.5 fusion.75
  43.7 0.3 fusion.6
  44.0 0.3 fusion.8
  44.4 0.3 fusion.10
  46.7 0.4 fusion.18
  47.1 0.4 fusion.19
  47.5 51.0 %all-gather.2.cloned.1.call-done = f32[512,2048]{1,0:T(8,128)} async-done(((f32[64,2048]{1,0:T(8,128)}), f32[512,2048]{1,0:T(8,128)}) %all-gather.2.cloned.1.call-update) | async-done | bytes 4194320 | tf_op jit(solution)/shard_map/all_gather | solution.py:42
  98.5 5.1 %convolution_bitcast_fusion = f32[16,8,512]{2,1,0:T(8,128)} fusion(f32[512,2048]{1,0:T(8,128)} %all-gather.2.cloned.1.call-done, f32[64,2048]{1,0:T(8,128)S(1)} %collective-permute-done, f32[64,2048]{1,0:T(8,128)S(1)} %bitcast.66, pred[]{:T(512)S(6)} %eq.63), kind=kOutput, calls=%fused_computation.1 | convolution fusion | flops 806092800 | bytes 5505025 | tf_op jit(solution)/shard_map/dot_general | solution.py:8
  103.6 9.0 %all-to-all-start.1 = ((f32[16,8,512]{2,1,0:T(8,128)}), f32[16,8,512]{2,1,0:T(8,128)S(1)}, u32[]{:S(2)}, u32[]{:S(2)}) async-start(f32[16,8,512]{2,1,0:T(8,128)} %convolution_bitcast_fusion), calls=%async_computation.1 | async-start | bytes 524288 | tf_op jit(solution)/shard_map/all_to_all | solution.py:61
  112.6 0.3 fusion.12
  112.9 0.4 fusion.20
  113.3 0.4 fusion.21
  113.7 10.7 %all-to-all-done.1 = f32[16,8,512]{2,1,0:T(8,128)S(1)} async-done(((f32[16,8,512]{2,1,0:T(8,128)}), f32[16,8,512]{2,1,0:T(8,128)S(1)}, u32[]{:S(2)}, u32[]{:S(2)}) %all-to-all-start.1) | async-done | bytes 262176 | tf_op jit(solution)/shard_map/all_to_all | solution.py:61
  124.6 0.3 fusion.49
  124.9 0.3 fusion.45
  125.5 14.5 %all_to_all.16 = f32[16,8,512]{2,1,0:T(8,128)S(1)} all-to-all(f32[16,8,512]{2,1,0:T(8,128)S(1)} %bitcast.67), channel_id=1, replica_groups={{0,128,256,384,512,640,768,896,8,136,264,392,520,648,776,904},{1,129,25..., dimensions={0} | all-to-all | bytes 524288 | tf_op jit(solution)/shard_map/all_to_all | solution.py:76
  140.0 3.6 %fusion.22 = f32[64,2048]{1,0:T(8,128)S(1)} fusion(f32[512,2048]{1,0:T(8,128)} %all-gather.2.cloned.1.call-done, f32[16,8,512]{2,1,0:T(8,128)S(1)} %all_to_all.16, pred[]{:T(512)S(6)} %eq.63), kind=kOutput, calls=%fused_computation.28 | convolution fusion | flops 402685952 | bytes 4980737 | tf_op jit(solution)/shard_map/dot_general | solution.py:8
  143.7 2.0 %collective-permute-start.1 = (f32[64,2048]{1,0:T(8,128)S(1)}, f32[64,2048]{1,0:T(8,128)S(1)}, u32[]{:S(2)}, u32[]{:S(2)}) collective-permute-start(f32[64,2048]{1,0:T(8,128)S(1)} %fusion.22), channel_id=1, source_target_pairs={{0,8},{1,9},{2,10},{3,11},{4,12},{5,13},{6,14},{7,15},{8,0},{9,1},... | collective-permute-start | bytes 1572872 | tf_op jit(solution)/shard_map/ppermute | solution.py:81
  145.7 1.6 convolution_add_fusion
  147.3 11.5 %collective-permute-done.1 = f32[64,2048]{1,0:T(8,128)S(1)} collective-permute-done((f32[64,2048]{1,0:T(8,128)S(1)}, f32[64,2048]{1,0:T(8,128)S(1)}, u32[]{:S(2)}, u32[]{:S(2)}) %collective-permute-start.1) | collective-permute-done | bytes 524320 | tf_op jit(solution)/shard_map/ppermute | solution.py:81
  158.8 0.9 add_bitcast_fusion
  (21 shorter events, 0.6 us)
Async XLA Ops:
  6.5 37.1 %copy-start = (f32[4,256,256]{2,1,0:T(8,128)S(1)}, f32[4,256,256]{2,1,0:T(8,128)}, u32[]{:S(2)}) copy-start(f32[4,256,256]{2,1,0:T(8,128)} %param.6) | copy-start | bytes 3145732
  6.5 92.0 %copy-start.2 = (f32[2048,64]{0,1:T(8,128)S(1)}, f32[2048,64]{0,1:T(8,128)}, u32[]{:S(2)}) copy-start(f32[2048,64]{0,1:T(8,128)} %param.4) | copy-start | bytes 1572868
  6.5 92.0 %all-gather.2.cloned.1.call-start = ((), (), s32[]{:S(2)}) async-start(), calls=%async_computation.3 | async-start | bytes 4718592 | tf_op jit(solution)/shard_map/all_gather | solution.py:42
  27.7 19.8 %collective-permute-start = (f32[64,2048]{1,0:T(8,128)}, f32[64,2048]{1,0:T(8,128)S(1)}, u32[]{:S(2)}, u32[]{:S(2)}) collective-permute-start(f32[64,2048]{1,0:T(8,128)} %bitcast.65), channel_id=1, source_target_pairs={{0,8},{1,9},{2,10},{3,11},{4,12},{5,13},{6,14},{7,15},{8,0},{9,1},... | collective-permute-start | bytes 1572872 | tf_op jit(solution)/shard_map/ppermute | solution.py:45
  103.6 20.8 %all-to-all-start.1 = ((f32[16,8,512]{2,1,0:T(8,128)}), f32[16,8,512]{2,1,0:T(8,128)S(1)}, u32[]{:S(2)}, u32[]{:S(2)}) async-start(f32[16,8,512]{2,1,0:T(8,128)} %convolution_bitcast_fusion), calls=%async_computation.1 | async-start | bytes 524288 | tf_op jit(solution)/shard_map/all_to_all | solution.py:61
  124.4 21.2 %copy-start.1 = (f32[512,2048]{1,0:T(8,128)S(1)}, f32[512,2048]{1,0:T(8,128)}, u32[]{:S(2)}) copy-start(f32[512,2048]{1,0:T(8,128)} %all-gather.2.cloned.1.call-done) | copy-start | bytes 12582916
  143.7 15.1 %collective-permute-start.1 = (f32[64,2048]{1,0:T(8,128)S(1)}, f32[64,2048]{1,0:T(8,128)S(1)}, u32[]{:S(2)}, u32[]{:S(2)}) collective-permute-start(f32[64,2048]{1,0:T(8,128)S(1)} %fusion.22), channel_id=1, source_target_pairs={{0,8},{1,9},{2,10},{3,11},{4,12},{5,13},{6,14},{7,15},{8,0},{9,1},... | collective-permute-start | bytes 1572872 | tf_op jit(solution)/shard_map/ppermute | solution.py:81
Sparse Core Ops, SparseCore 0:
  27.8 70.6 all-gather.1

commit v3 on v2

v3 whole, which is shorter than its diff:
```python
import jax
import jax.numpy as jnp
from jax import lax
from jax.sharding import PartitionSpec as P

BOTH = ("pw", "band")
CORES = 2


def dot(a, b, dims, precision=lax.Precision.HIGH):
    return lax.dot_general(
        a, b, (dims, ((), ())), precision=precision, preferred_element_type=jnp.float32
    )


def make_local(npw, nx, nzl, ny):
    side, nband = nx, nx * nzl * ny

    def at(pw, x, z, y):
        return pw * nband + (x * nzl + z) * ny + y

    def lines(last):
        groups = []
        for pw in range(npw):
            along_x = (pw % CORES == 0) == last
            for z in range(nzl):
                for fixed in range(side):
                    groups.append(
                        [at(pw, i, z, fixed) if along_x else at(pw, fixed, z, i) for i in range(side)]
                    )
        return groups

    column = [
        [at(pw, x, z, y) for z in range(nzl) for pw in range(npw)]
        for x in range(nx)
        for y in range(ny)
    ]
    swap = [
        (at(pw, x, z, y), at(pw, x, z ^ 1, y))
        for pw in range(npw)
        for x in range(nx)
        for z in range(nzl)
        for y in range(ny)
    ]

    def gather(piece, last):
        spread = jnp.broadcast_to(piece[None], (side,) + piece.shape)
        got = lax.all_to_all(spread, BOTH, 0, 0, axis_index_groups=lines(last))
        return got.reshape(side * piece.shape[0], piece.shape[1])

    def local(wavefunctions, projectors, coupling, block_type):
        block = coupling.shape[1]
        nblocks = block_type.shape[0]
        wt = wavefunctions.T
        pt = projectors.T
        bands, rows = wt.shape
        mine = pt.shape[0]
        place = lax.axis_index("band")
        first = (place // ny) % nzl == 0
        core = lax.axis_index("pw") % CORES
        members = nzl * npw
        half = rows // 2
        held = side * side * mine

        line = gather(pt, False)
        gathered = gather(line, True)
        _, wt_out = lax.optimization_barrier((line, wt))
        other = lax.ppermute(wt_out, BOTH, swap)
        pair = jnp.where(first, jnp.concatenate([wt, other]), jnp.concatenate([other, wt]))

        spot = jnp.arange(held, dtype=jnp.int32)
        outer, inner, j = spot // (side * mine), (spot // mine) % side, spot % mine
        shared = jnp.where(core == 0, spot, (inner * side + outer) * mine + j)
        order = (shared[:, None] == spot[None, :]).astype(jnp.float32)

        piece = block // nzl
        b_at = jnp.arange(block, dtype=jnp.int32)
        z, out_at, in_at = b_at // piece, (b_at % piece) // (ny * mine), b_at % (ny * mine)
        source = (out_at * nzl + z) * (ny * mine) + in_at
        pick = (source[:, None] == b_at[None, :]).astype(jnp.float32)
        mixers = []
        for i in range(nblocks):
            v = lax.dynamic_index_in_dim(coupling, block_type[i], 0, keepdims=False)
            v = dot(pick, v, ((1,), (0,)), lax.Precision.HIGHEST)
            mixers.append(dot(v, pick, ((1,), (1,)), lax.Precision.HIGHEST))
        pair, *mixers = lax.optimization_barrier((pair, *mixers))

        part = dot(pair, gathered, ((1,), (1,)))
        part = dot(part, order, ((1,), (0,)), lax.Precision.HIGHEST)
        few = nzl * bands // members
        split = lax.all_to_all(
            part.reshape(members, few, held), BOTH, 0, 0, axis_index_groups=column
        )
        proj = jnp.sum(split.reshape(nzl, npw, few, held), axis=1)
        coupled = []
        for i in range(nblocks):
            own = [proj[z, :, i * piece : (i + 1) * piece] for z in range(nzl)]
            coupled.append(dot(jnp.concatenate(own, axis=1), mixers[i], ((1,), (1,))))
        back = jnp.stack(
            [
                jnp.concatenate([c[:, z * piece : (z + 1) * piece] for c in coupled], axis=1)
                for z in range(nzl)
            ]
        )
        back = jnp.broadcast_to(back[:, None], (nzl, npw, few, held)).reshape(members, few, held)
        full = lax.all_to_all(back, BOTH, 0, 0, axis_index_groups=column).reshape(
            nzl * bands, held
        )
        full = dot(full, order, ((1,), (1,)), lax.Precision.HIGHEST)
        low, high = full[:bands], full[bands:]
        away, home = jnp.where(first, high, low), jnp.where(first, low, high)
        cuts = [gathered[:, :half], gathered[:, half:]]
        received = [lax.ppermute(dot(away, g, ((1,), (0,))), BOTH, swap) for g in cuts]
        kept = [
            wt[:, h * half : (h + 1) * half] + dot(home, g, ((1,), (0,)))
            for h, g in enumerate(cuts)
        ]
        kept = lax.optimization_barrier(kept)
        return jnp.concatenate([k + r for k, r in zip(kept, received)], axis=1).T

    return local


def solution(mesh):
    local = make_local(mesh.shape["pw"], 8, 2, 8)
    return jax.shard_map(
        local,
        mesh=mesh,
        in_specs=(P("pw", "band"), P("pw", "band"), P(), P()),
        out_specs=P("pw", "band"),
        check_vma=False,
    )
```

time: 167 us -> 159 us (0.952)
  waiting for transfers between devices: 73.2 us -> 41.6 us
  blocking collectives: 34.6 us -> 65.2 us
  between operations: 21.2 us -> 7.41 us
  matrix products: 14.2 us -> 19.7 us
  starting transfers between devices: 19.8 us -> 17.8 us
    all_gather x1 -> x0, waiting for transfers between devices: 51 us -> none  [local(): lax.all_gather(line, 'band', axis=0, axis_index_groups=along_x, tiled=True)]
    all_to_all x2 -> x3, blocking collectives: 34.6 us -> 65.2 us  [the longest x1 31.9 us: local(): lax.all_to_all(part.reshape(members, few, held), BOTH, 0, 0, axis_index_g...]
    all_to_all x1, waiting for transfers between devices: 10.7 us -> 34.2 us  [gather(): got = lax.all_to_all(spread, BOTH, 0, 0, axis_index_groups=lines(last))]
    dot_general x15 -> x19, matrix products: 14.2 us -> 19.7 us  [dot(): lax.dot_general(a, b, (dims, ((), ())), precision=precision, preferred_el...]
    ppermute x2 -> x3, waiting for transfers between devices: 11.5 us -> 7.42 us  [the longest x2 7.42 us: local(): lax.ppermute(dot(away, g, ((1,), (0,))), BOTH, swap)]
    broadcast_in_dim x1 -> x2, local copies, waits for them, and re-layouts: 0.99 us -> 3.45 us  [gather(): spread = jnp.broadcast_to(piece[None], (side,) + piece.shape)]
    ppermute x2 -> x3, starting transfers between devices: 10.9 us -> 10.2 us  [the longest x2 5.28 us: local(): lax.ppermute(dot(away, g, ((1,), (0,))), BOTH, swap)]
  transfers between devices with their start and end apart: 4 -> 4, of which waited for: 3 -> 3; matrix products, arithmetic and copies ran while one was open for 4% -> 5% of each run, Pallas kernels for 0% -> 0%
where the time goes in v3:
time: 159 us; the launch traced here: 158 us
  blocking collectives  65.2 us (41%)
  waiting for transfers between devices  41.6 us (26%)
  matrix products  19.7 us (12%)
  starting transfers between devices  17.8 us (11%)
  between operations  7.41 us (5%)
  local copies, waits for them, and re-layouts  4.11 us (3%)
  other arithmetic  2.3 us (1%)
    all_to_all x1, waiting for transfers between devices, gather(): got = lax.all_to_all(spread, BOTH, 0, 0, axis_index_groups=lines(last))  34.2 us
    all_to_all x1, blocking collectives, local(): lax.all_to_all(part.reshape(members, few, held), BOTH, 0, 0, axis_index_g...  31.9 us
    dot_general x19, matrix products, dot(): lax.dot_general(a, b, (dims, ((), ())), precision=precision, preferred_el...  19.7 us
    all_to_all x1, blocking collectives, gather(): got = lax.all_to_all(spread, BOTH, 0, 0, axis_index_groups=lines(last))  19 us
    all_to_all x1, blocking collectives, local(): lax.all_to_all(back, BOTH, 0, 0, axis_index_groups=column)  14.4 us
    all_to_all x1, starting transfers between devices, gather(): got = lax.all_to_all(spread, BOTH, 0, 0, axis_index_groups=lines(last))  7.65 us
    ppermute x2, waiting for transfers between devices, local(): lax.ppermute(dot(away, g, ((1,), (0,))), BOTH, swap)  7.42 us
    ppermute x2, starting transfers between devices, local(): lax.ppermute(dot(away, g, ((1,), (0,))), BOTH, swap)  5.28 us
  transfers between devices with their start and end apart: 4, of which 3 were waited for; matrix products, arithmetic and copies ran while one was open for 5% of the time, Pallas kernels for 0%

profile of v3, /device:TPU:1, one launch (start us, length us, event | category | flops | bytes accessed | tf_op | source)
XLA Modules:
  0.0 158.2 jit_solution(5816597154648667680)
XLA Ops:
  0.0 1.0 broadcast_in_dim.8
  1.0 19.0 %all_to_all.20 = f32[8,8,2048]{2,1,0:T(8,128)S(1)} all-to-all(f32[8,8,2048]{2,1,0:T(8,128)S(1)} %broadcast_in_dim.8), channel_id=1, replica_groups={{0,1,2,3,4,5,6,7},{16,17,18,19,20,21,22,23},{32,33,34,35,36,37,38,39},{..., dimensions={0} | all-to-all | bytes 1048576 | tf_op jit(solution)/shard_map/all_to_all | solution.py:48
  20.0 2.5 %broadcast_in_dim.10 = f32[8,64,2048]{2,1,0:T(8,128)} broadcast(f32[64,2048]{1,0:T(8,128)S(1)} %bitcast.65), dimensions={1,2} | broadcast | bytes 4718592 | tf_op jit(solution)/shard_map/broadcast_in_dim | solution.py:47
  22.5 7.6 %all-to-all-start.1 = ((f32[8,64,2048]{2,1,0:T(8,128)}), f32[8,64,2048]{2,1,0:T(8,128)}, u32[]{:S(2)}, u32[]{:S(2)}) async-start(f32[8,64,2048]{2,1,0:T(8,128)} %broadcast_in_dim.10), calls=%async_computation.1 | async-start | bytes 8388608 | tf_op jit(solution)/shard_map/all_to_all | solution.py:48
  30.1 4.9 %collective-permute-start = (f32[64,2048]{1,0:T(8,128)S(1)}, f32[64,2048]{1,0:T(8,128)}, u32[]{:S(2)}, u32[]{:S(2)}) collective-permute-start(f32[64,2048]{1,0:T(8,128)S(1)} %bitcast.61), channel_id=1, source_target_pairs={{0,8},{1,9},{2,10},{3,11},{4,12},{5,13},{6,14},{7,15},{8,0},{9,1},... | collective-permute-start | bytes 1572872 | tf_op jit(solution)/shard_map/ppermute | solution.py:68
  35.0 0.6 fusion.89
  44.6 0.4 fusion.32
  45.5 1.1 fusion.30
  46.6 1.3 maximum_select_fusion
  47.9 34.2 %all-to-all-done.1 = f32[8,64,2048]{2,1,0:T(8,128)} async-done(((f32[8,64,2048]{2,1,0:T(8,128)}), f32[8,64,2048]{2,1,0:T(8,128)}, u32[]{:S(2)}, u32[]{:S(2)}) %all-to-all-start.1) | async-done | bytes 4194336 | tf_op jit(solution)/shard_map/all_to_all | solution.py:48
  82.1 4.4 %fusion.90 = f32[128,512]{1,0:T(8,128)S(1)} fusion(f32[128,2048]{1,0:T(8,128)S(1)} %maximum_select_fusion, f32[512,2048]{1,0:T(8,128)} %bitcast.11), kind=kOutput, calls=%fused_computation.126 | convolution fusion | flops 805306368 | bytes 5505024 | tf_op jit(solution)/shard_map/dot_general | solution.py:11
  86.5 0.6 convolution_bitcast_fusion
  87.1 31.9 %all_to_all.21 = f32[16,8,512]{2,1,0:T(8,128)S(1)} all-to-all(f32[16,8,512]{2,1,0:T(8,128)S(1)} %convolution_bitcast_fusion), channel_id=1, replica_groups={{0,128,256,384,512,640,768,896,8,136,264,392,520,648,776,904},{1,129,25..., dimensions={0} | all-to-all | bytes 524288 | tf_op jit(solution)/shard_map/all_to_all | solution.py:91
  120.1 14.4 %all_to_all.22 = f32[16,8,512]{2,1,0:T(8,128)S(1)} all-to-all(f32[16,8,512]{2,1,0:T(8,128)S(1)} %bitcast.66), channel_id=1, replica_groups={{0,128,256,384,512,640,768,896,8,136,264,392,520,648,776,904},{1,129,25..., dimensions={0} | all-to-all | bytes 524288 | tf_op jit(solution)/shard_map/all_to_all | solution.py:106
  134.5 0.8 fusion.14
  135.2 2.3 %fusion.8 = f32[64,1024]{1,0:T(8,128)S(1)} fusion(f32[512,2048]{1,0:T(8,128)} %bitcast.11, f32[64,2048]{1,0:T(8,128)S(1)} %bitcast.63, f32[128,512]{1,0:T(8,128)S(1)} %fusion.14, pred[]{:T(512)S(6)} %eq.83), kind=kOutput, calls=%fused_computation.8 | convolution fusion | flops 201424896 | bytes 2883585 | tf_op jit(solution)/shard_map/dot_general | solution.py:11
  137.6 2.3 %fusion = f32[64,1024]{1,0:T(8,128)S(1)} fusion(f32[512,2048]{1,0:T(8,128)} %bitcast.11, f32[128,512]{1,0:T(8,128)S(1)} %fusion.14, pred[]{:T(512)S(6)} %eq.83), kind=kOutput, calls=%fused_computation | convolution fusion | flops 201359360 | bytes 2621441 | tf_op jit(solution)/shard_map/dot_general | solution.py:11
  139.9 2.3 %fusion.4 = f32[64,1024]{1,0:T(8,128)S(1)} fusion(f32[512,2048]{1,0:T(8,128)} %bitcast.11, f32[128,512]{1,0:T(8,128)S(1)} %fusion.14, pred[]{:T(512)S(6)} %eq.83), kind=kOutput, calls=%fused_computation.4 | convolution fusion | flops 201359360 | bytes 2621441 | tf_op jit(solution)/shard_map/dot_general | solution.py:11
  142.3 2.0 %collective-permute-start.2 = (f32[64,1024]{1,0:T(8,128)S(1)}, f32[64,1024]{1,0:T(8,128)S(1)}, u32[]{:S(2)}, u32[]{:S(2)}) collective-permute-start(f32[64,1024]{1,0:T(8,128)S(1)} %fusion), channel_id=1, source_target_pairs={{0,8},{1,9},{2,10},{3,11},{4,12},{5,13},{6,14},{7,15},{8,0},{9,1},... | collective-permute-start | bytes 786440 | tf_op jit(solution)/shard_map/ppermute | solution.py:113
  144.3 3.3 %collective-permute-start.1 = (f32[64,1024]{1,0:T(8,128)S(1)}, f32[64,1024]{1,0:T(8,128)S(1)}, u32[]{:S(2)}, u32[]{:S(2)}) collective-permute-start(f32[64,1024]{1,0:T(8,128)S(1)} %fusion.4), channel_id=1, source_target_pairs={{0,8},{1,9},{2,10},{3,11},{4,12},{5,13},{6,14},{7,15},{8,0},{9,1},... | collective-permute-start | bytes 786440 | tf_op jit(solution)/shard_map/ppermute | solution.py:113
  147.6 2.3 %fusion.11 = f32[64,1024]{1,0:T(8,128)S(1)} fusion(f32[512,2048]{1,0:T(8,128)} %bitcast.11, f32[64,2048]{1,0:T(8,128)S(1)} %bitcast.64, f32[128,512]{1,0:T(8,128)S(1)} %fusion.14, pred[]{:T(512)S(6)} %eq.83), kind=kOutput, calls=%fused_computation.9 | convolution fusion | flops 201424896 | bytes 2883585 | tf_op jit(solution)/shard_map/dot_general | solution.py:11
  149.9 2.6 %collective-permute-done.2 = f32[64,1024]{1,0:T(8,128)S(1)} collective-permute-done((f32[64,1024]{1,0:T(8,128)S(1)}, f32[64,1024]{1,0:T(8,128)S(1)}, u32[]{:S(2)}, u32[]{:S(2)}) %collective-permute-start.2) | collective-permute-done | bytes 262176 | tf_op jit(solution)/shard_map/ppermute | solution.py:113
  152.5 4.8 %collective-permute-done.1 = f32[64,1024]{1,0:T(8,128)S(1)} collective-permute-done((f32[64,1024]{1,0:T(8,128)S(1)}, f32[64,1024]{1,0:T(8,128)S(1)}, u32[]{:S(2)}, u32[]{:S(2)}) %collective-permute-start.1) | collective-permute-done | bytes 262176 | tf_op jit(solution)/shard_map/ppermute | solution.py:113
  157.4 0.8 maximum_bitcast_fusion
  (32 shorter events, 3.3 us)
Async XLA Ops:
  0.0 42.8 %copy-start = (f32[4,256,256]{2,1,0:T(8,128)S(1)}, f32[4,256,256]{2,1,0:T(8,128)}, u32[]{:S(2)}) copy-start(f32[4,256,256]{2,1,0:T(8,128)} %param.6) | copy-start | bytes 3145732
  22.5 7.7 %copy-start.1 = (f32[2048,64]{0,1:T(8,128)S(1)}, f32[2048,64]{0,1:T(8,128)}, u32[]{:S(2)}) copy-start(f32[2048,64]{0,1:T(8,128)} %param.4) | copy-start | bytes 1572868
  22.5 12.6 %copy-start.3 = (s32[4]{0:T(128)S(1)}, s32[4]{0:T(128)}, u32[]{:S(2)}) copy-start(s32[4]{0:T(128)} %param.7) | copy-start | bytes 52
  22.5 59.6 %all-to-all-start.1 = ((f32[8,64,2048]{2,1,0:T(8,128)}), f32[8,64,2048]{2,1,0:T(8,128)}, u32[]{:S(2)}, u32[]{:S(2)}) async-start(f32[8,64,2048]{2,1,0:T(8,128)} %broadcast_in_dim.10), calls=%async_computation.1 | async-start | bytes 8388608 | tf_op jit(solution)/shard_map/all_to_all | solution.py:48
  30.1 16.5 %collective-permute-start = (f32[64,2048]{1,0:T(8,128)S(1)}, f32[64,2048]{1,0:T(8,128)}, u32[]{:S(2)}, u32[]{:S(2)}) collective-permute-start(f32[64,2048]{1,0:T(8,128)S(1)} %bitcast.61), channel_id=1, source_target_pairs={{0,8},{1,9},{2,10},{3,11},{4,12},{5,13},{6,14},{7,15},{8,0},{9,1},... | collective-permute-start | bytes 1572872 | tf_op jit(solution)/shard_map/ppermute | solution.py:68
  82.1 36.9 %copy-start.2 = (f32[256,256]{1,0:T(8,128)S(1)}, f32[256,256]{1,0:T(8,128)}, u32[]{:S(2)}) copy-start(f32[256,256]{1,0:T(8,128)} %fusion.30) | copy-start | bytes 786436
  142.3 10.2 %collective-permute-start.2 = (f32[64,1024]{1,0:T(8,128)S(1)}, f32[64,1024]{1,0:T(8,128)S(1)}, u32[]{:S(2)}, u32[]{:S(2)}) collective-permute-start(f32[64,1024]{1,0:T(8,128)S(1)} %fusion), channel_id=1, source_target_pairs={{0,8},{1,9},{2,10},{3,11},{4,12},{5,13},{6,14},{7,15},{8,0},{9,1},... | collective-permute-start | bytes 786440 | tf_op jit(solution)/shard_map/ppermute | solution.py:113
  144.3 13.1 %collective-permute-start.1 = (f32[64,1024]{1,0:T(8,128)S(1)}, f32[64,1024]{1,0:T(8,128)S(1)}, u32[]{:S(2)}, u32[]{:S(2)}) collective-permute-start(f32[64,1024]{1,0:T(8,128)S(1)} %fusion.4), channel_id=1, source_target_pairs={{0,8},{1,9},{2,10},{3,11},{4,12},{5,13},{6,14},{7,15},{8,0},{9,1},... | collective-permute-start | bytes 786440 | tf_op jit(solution)/shard_map/ppermute | solution.py:113
